TPU v7x, 32 devices: a whole 2x2x4 slice. The times are simulated.
32 devices in a mesh: blk: 8 (over y, x, core), team: 4 (over z).
Axes of the slice: x: 2, y: 2, z: 4, core: 2. Of those that a mesh axis runs over, the one named last changes fastest.
Arguments:
- features: bfloat16 [8192, 128], P(('blk', 'team')), may hold values from -0.796875 to 0.796875
- left_vectors: bfloat16 [8192, 128], P(('blk', 'team')), may hold values from -0.8984375 to 0.8984375
- right_vectors: bfloat16 [8192, 128], P(('blk', 'team')), may hold values from -0.8984375 to 0.8984375
Outputs:
- feature_grad: float32 [8192, 128], P(('blk', 'team'))
All inputs are finite; a program needn't handle non-finite values.
Results may differ from a plain program's by a relative error of at most 0.0039.
Values may be sent and summed in bfloat16 or wider, within the bound.
A program may use at most 64 MiB of HBM per device.

v0:
```python
import jax
import jax.numpy as jnp
from jax import lax
from jax.sharding import PartitionSpec as P


def pair_block(targets, source_x, source_l, source_r):
    target_x, target_l, target_r, target_norm = targets
    source_norm = jnp.sum(source_x.astype(jnp.float32) ** 2, axis=1)
    cross = jnp.einsum("if,jf->ij", target_x, source_x, preferred_element_type=jnp.float32)
    dist_sq = target_norm[:, None] + source_norm[None, :] - 2.0 * cross
    radius = jnp.sqrt(jnp.maximum(dist_sq, 0.0))
    couple = jnp.einsum(
        "iv,jv->ij", target_l, source_r, preferred_element_type=jnp.float32
    ) + jnp.einsum("iv,jv->ij", target_r, source_l, preferred_element_type=jnp.float32)
    root_five = jnp.float32(5.0) ** 0.5
    weight = (
        -(5.0 / 3.0) * (1.0 + root_five * radius) * jnp.exp(-root_five * radius) * couple
    ).astype(jnp.bfloat16)
    row_total = jnp.sum(weight.astype(jnp.float32), axis=1)
    return row_total[:, None] * target_x.astype(jnp.float32) - jnp.dot(
        weight, source_x, preferred_element_type=jnp.float32
    )


def sweep_sources(running, targets, pieces):
    source_x, source_l, source_r = pieces
    count_rows = source_x.shape[0]
    count_blocks = count_rows // 512

    def one_step(accum, packed):
        return (accum + pair_block(targets, packed[0], packed[1], packed[2]), None)

    stacked = (
        source_x.reshape(count_blocks, 512, -1),
        source_l.reshape(count_blocks, 512, -1),
        source_r.reshape(count_blocks, 512, -1),
    )
    running, unused = lax.scan(one_step, running, stacked)
    return running


def with_norms(target_x, target_l, target_r):
    return (target_x, target_l, target_r, jnp.sum(target_x.astype(jnp.float32) ** 2, axis=1))


def local(features, left_vectors, right_vectors):
    block_x, block_l, block_r = (
        lax.all_gather(features, "team", axis=0, tiled=True),
        lax.all_gather(left_vectors, "team", axis=0, tiled=True),
        lax.all_gather(right_vectors, "team", axis=0, tiled=True),
    )
    targets = with_norms(block_x, block_l, block_r)
    start_grad = jnp.zeros(block_x.shape, jnp.float32)
    partial_value = sweep_sources(
        start_grad,
        targets,
        (
            lax.all_gather(features, "blk", axis=0, tiled=True),
            lax.all_gather(left_vectors, "blk", axis=0, tiled=True),
            lax.all_gather(right_vectors, "blk", axis=0, tiled=True),
        ),
    )
    return lax.psum_scatter(partial_value, "team", scatter_dimension=0, tiled=True)


def solution(mesh):
    in_specs = (P(("blk", "team"), None), P(("blk", "team"), None), P(("blk", "team"), None))
    out_specs = P(("blk", "team"), None)
    return jax.shard_map(local, mesh=mesh, in_specs=in_specs, out_specs=out_specs, check_vma=False)
```

profile of v0, /device:TPU:0, one launch (start us, length us, event | category | flops | bytes accessed | tf_op | source)
XLA Modules:
  0.0 129.7 jit_solution(12730551391967824644)
XLA Ops:
  6.5 0.0 copy-start.1
  6.5 0.0 reduce-scatter.2.cloned.1.call-start
  6.5 16.0 %all_gather.18 = bf16[1024,128]{1,0:T(8,128)(2,1)S(1)} all-gather(bf16[256,128]{1,0:T(8,128)(2,1)} %param.5), channel_id=1, replica_groups=mesh['blk'=8,'team'=4] {'team'}, dimensions={0}, use_global_device_ids=true | all-gather | bytes 327680 | tf_op jit(solution)/shard_map/all_gather | solution.py:49
  22.5 10.1 %all_gather.19 = bf16[2048,128]{1,0:T(8,128)(2,1)S(1)} all-gather(bf16[256,128]{1,0:T(8,128)(2,1)} %param.5), channel_id=1, replica_groups=mesh['blk'=8,'team'=4] {'blk'}, dimensions={0}, use_global_device_ids=true | all-gather | bytes 589824 | tf_op jit(solution)/shard_map/all_gather | solution.py:59
  32.7 10.8 %all_gather.22 = bf16[2048,128]{1,0:T(8,128)(2,1)} all-gather(bf16[256,128]{1,0:T(8,128)(2,1)} %param.6), channel_id=1, replica_groups=mesh['blk'=8,'team'=4] {'blk'}, dimensions={0}, use_global_device_ids=true | all-gather | bytes 589824 | tf_op jit(solution)/shard_map/all_gather | solution.py:60
  43.4 14.5 %all_gather.21 = bf16[1024,128]{1,0:T(8,128)(2,1)S(1)} all-gather(bf16[256,128]{1,0:T(8,128)(2,1)} %param.6), channel_id=1, replica_groups=mesh['blk'=8,'team'=4] {'team'}, dimensions={0}, use_global_device_ids=true | all-gather | bytes 327680 | tf_op jit(solution)/shard_map/all_gather | solution.py:50
  57.9 9.5 %all_gather.20 = bf16[2048,128]{1,0:T(8,128)(2,1)S(1)} all-gather(bf16[256,128]{1,0:T(8,128)(2,1)} %param.7), channel_id=1, replica_groups=mesh['blk'=8,'team'=4] {'blk'}, dimensions={0}, use_global_device_ids=true | all-gather | bytes 589824 | tf_op jit(solution)/shard_map/all_gather | solution.py:61
  67.5 0.0 copy-done.1
  67.5 14.5 %all_gather.23 = bf16[1024,128]{1,0:T(8,128)(2,1)S(1)} all-gather(bf16[256,128]{1,0:T(8,128)(2,1)S(1)} %copy-done.1), channel_id=1, replica_groups=mesh['blk'=8,'team'=4] {'team'}, dimensions={0}, use_global_device_ids=true | all-gather | bytes 327680 | tf_op jit(solution)/shard_map/all_gather | solution.py:51
  81.9 0.2 multiply_reduce_fusion.1
  82.1 17.1 %while.13 = (s32[]{:T(128)}, f32[1024,128]{1,0:T(8,128)S(1)}, f32[1024]{0:T(1024)S(1)}, bf16[4,512,128]{2,1,0:T(8,128)(2,1)S(1)}, bf16[1024,128]{1,0:T(8,128)(2,...) while((s32[]{:T(128)}, f32[1024,128]{1,0:T(8,128)S(1)}, ...), condition=%wide.region_4.5_spmd.clone, body=%wide.region_1.4_spmd.clone.sunk | while | flops 545061376 | bytes 13255303 | solution.py:39
  82.1 0.4 fusion.40
  82.6 0.2 multiply_reduce_fusion.3
  82.7 0.4 fusion.39
  83.2 2.5 %convert_reduce_fusion.2 = (f32[1024]{0:T(1024)S(1)}, bf16[1024,512]{0,1:T(8,128)(2,1)S(1)}) fusion(f32[512,1024]{1,0:T(8,128)S(1)} %fusion.39, bf16[1024,128]{1,0:T(8,128)(2,1)S(1)} %get-tuple-element.259, bf16[4,512,128]{2,1,0:T(8,128)(2,1)} %get-tuple-element.258, s32[]{:T(128)} %get-tuple-element.240, f32[512,1024]{1,0:T(8,128)S(1)} %fusion.40, ...), kind=kOutput, calls=%fused_computation.5.clone.1 | convolution fusion | flops 141556736 | bytes 5646848 | tf_op jit(solution)/shard_map/while/body/eval_jaxpr/iv,jv->ij/dot_general | solution.py:15
  85.7 0.7 fusion.41
  86.4 0.4 fusion.40
  86.9 0.2 multiply_reduce_fusion.3
  87.0 0.4 fusion.39
  87.5 2.5 %convert_reduce_fusion.2 = (f32[1024]{0:T(1024)S(1)}, bf16[1024,512]{0,1:T(8,128)(2,1)S(1)}) fusion(f32[512,1024]{1,0:T(8,128)S(1)} %fusion.39, bf16[1024,128]{1,0:T(8,128)(2,1)S(1)} %get-tuple-element.259, bf16[4,512,128]{2,1,0:T(8,128)(2,1)} %get-tuple-element.258, s32[]{:T(128)} %get-tuple-element.240, f32[512,1024]{1,0:T(8,128)S(1)} %fusion.40, ...), kind=kOutput, calls=%fused_computation.5.clone.1 | convolution fusion | flops 141556736 | bytes 5646848 | tf_op jit(solution)/shard_map/while/body/eval_jaxpr/iv,jv->ij/dot_general | solution.py:15
  90.0 0.7 fusion.41
  90.7 0.4 fusion.40
  91.1 0.2 multiply_reduce_fusion.3
  91.3 0.4 fusion.39
  91.7 2.5 %convert_reduce_fusion.2 = (f32[1024]{0:T(1024)S(1)}, bf16[1024,512]{0,1:T(8,128)(2,1)S(1)}) fusion(f32[512,1024]{1,0:T(8,128)S(1)} %fusion.39, bf16[1024,128]{1,0:T(8,128)(2,1)S(1)} %get-tuple-element.259, bf16[4,512,128]{2,1,0:T(8,128)(2,1)} %get-tuple-element.258, s32[]{:T(128)} %get-tuple-element.240, f32[512,1024]{1,0:T(8,128)S(1)} %fusion.40, ...), kind=kOutput, calls=%fused_computation.5.clone.1 | convolution fusion | flops 141556736 | bytes 5646848 | tf_op jit(solution)/shard_map/while/body/eval_jaxpr/iv,jv->ij/dot_general | solution.py:15
  94.3 0.7 fusion.41
  95.0 0.4 fusion.40
  95.4 0.2 multiply_reduce_fusion.3
  95.6 0.4 fusion.39
  96.0 2.5 %convert_reduce_fusion.2 = (f32[1024]{0:T(1024)S(1)}, bf16[1024,512]{0,1:T(8,128)(2,1)S(1)}) fusion(f32[512,1024]{1,0:T(8,128)S(1)} %fusion.39, bf16[1024,128]{1,0:T(8,128)(2,1)S(1)} %get-tuple-element.259, bf16[4,512,128]{2,1,0:T(8,128)(2,1)} %get-tuple-element.258, s32[]{:T(128)} %get-tuple-element.240, f32[512,1024]{1,0:T(8,128)S(1)} %fusion.40, ...), kind=kOutput, calls=%fused_computation.5.clone.1 | convolution fusion | flops 141556736 | bytes 5646848 | tf_op jit(solution)/shard_map/while/body/eval_jaxpr/iv,jv->ij/dot_general | solution.py:15
  98.6 0.7 fusion.41
  99.3 0.0 copy-start
  99.3 0.8 copy-done
  100.0 0.0 reduce-scatter.2.cloned.1.call-update
  100.1 22.8 %reduce-scatter.2.cloned.1.call-done = f32[256,128]{1,0:T(8,128)} async-done(((f32[1024,128]{1,0:T(8,128)}), f32[256,128]{1,0:T(8,128)}) %reduce-scatter.2.cloned.1.call-update) | async-done | bytes 131088 | tf_op jit(solution)/shard_map/reduce_scatter | solution.py:64
  (1 shorter events, 0.0 us)
Async XLA Ops:
  6.5 60.9 %copy-start.1 = (bf16[256,128]{1,0:T(8,128)(2,1)S(1)}, bf16[256,128]{1,0:T(8,128)(2,1)}, u32[]{:S(2)}) copy-start(bf16[256,128]{1,0:T(8,128)(2,1)} %param.7) | copy-start | bytes 196612
  6.5 116.3 %reduce-scatter.2.cloned.1.call-start = ((), (), s32[]{:S(2)}) async-start(), calls=%async_computation.1 | async-start | bytes 655360 | tf_op jit(solution)/shard_map/reduce_scatter | solution.py:64
  99.3 0.8 copy-start
Sparse Core Ops, SparseCore 0:
  100.2 22.6 reduce-scatter.1
where the time goes:
time: 130 us
  blocking collectives  75.4 us (58%)
  waiting for transfers between devices  22.8 us (18%)
  matrix products  16.3 us (13%)
  between operations  13.4 us (10%)
    reduce_scatter x1, waiting for transfers between devices, local(): lax.psum_scatter(partial_value, 'team', scatter_dimension=0, tiled=True)  22.8 us
    all_gather x1, blocking collectives, local(): lax.all_gather(features, 'team', axis=0, tiled=True)  16 us
    all_gather x1, blocking collectives, local(): lax.all_gather(left_vectors, 'team', axis=0, tiled=True)  14.5 us
    all_gather x1, blocking collectives, local(): lax.all_gather(right_vectors, 'team', axis=0, tiled=True)  14.5 us
    all_gather x1, blocking collectives, local(): lax.all_gather(left_vectors, 'blk', axis=0, tiled=True)  10.8 us
    dot_general x4, matrix products, pair_block(): jnp.einsum('iv,jv->ij', target_r, source_l, preferred_element_type=jnp.fl...  10.1 us
    all_gather x1, blocking collectives, local(): lax.all_gather(features, 'blk', axis=0, tiled=True)  10.1 us
    all_gather x1, blocking collectives, local(): lax.all_gather(right_vectors, 'blk', axis=0, tiled=True)  9.53 us
  transfers between devices with their start and end apart: 1, of which 1 were waited for; matrix products, arithmetic and copies ran while one was open for 0% of the time, Pallas kernels for 0%

commit v1 on v0

v1 whole, which is shorter than its diff:
```python
import functools
import math

import jax
import jax.numpy as jnp
from jax import lax
from jax.experimental import pallas as pl
from jax.experimental.pallas import tpu as pltpu
from jax.sharding import PartitionSpec as P

MESH = pl.DeviceIdType.MESH
LOG2E = math.log2(math.e)
RATE = math.sqrt(5.0) * LOG2E
GAIN = -(5.0 / 3.0) / LOG2E
NT = (((1,), (1,)), ((), ()))


def flip(index, bits):
    step = 1
    while step <= bits:
        if bits & step:
            index = index + step - 2 * step * ((index // step) % 2)
        step *= 2
    return index


def columns(norm, lane, first, ones):
    high = norm.astype(jnp.bfloat16).astype(jnp.float32)
    rest = norm - high
    mid = rest.astype(jnp.bfloat16).astype(jnp.float32)
    low = rest - mid
    out = jnp.where((lane >= ones) & (lane < ones + 3), 1.0, 0.0)
    for place, term in enumerate((high, mid, low)):
        out = jnp.where(lane == first + place, term, out)
    return out.astype(jnp.bfloat16)


def kernel(
    planes, teams, tile, x_hbm, l_hbm, r_hbm, out_ref,
    own, tgt, src, tgt_aug, src_aug, acc, grad_out, grad_in,
    load_sem, tgt_send, tgt_recv, z_send, z_recv, p_send, p_recv, g_send, g_recv,
):
    blk, team = lax.axis_index("blk"), lax.axis_index("team")
    plane, core = blk // 2, blk % 2
    rows, feat = x_hbm.shape

    loads = [
        pltpu.make_async_copy(ref, own.at[i], load_sem.at[i])
        for i, ref in enumerate((x_hbm, l_hbm, r_hbm))
    ]
    for load in loads:
        load.start()

    partner = (plane * 2 + 1 - core, team)
    plane_peer = [(flip(plane, k) * 2 + core, team) for k in range(planes)]
    team_peer = [(blk, flip(team, k)) for k in range(teams)]
    peers = [partner] + plane_peer[1:] + team_peer[1:]
    barrier = pltpu.get_barrier_semaphore()
    for peer in peers:
        pl.semaphore_signal(barrier, inc=1, device_id=peer, device_id_type=MESH)

    def remote(source, target, send, recv, peer):
        return pltpu.make_async_remote_copy(
            src_ref=source, dst_ref=target, send_sem=send, recv_sem=recv,
            device_id=peer, device_id_type=MESH,
        )

    to_plane = [None] + [
        remote(own, tgt.at[k - 1], tgt_send.at[k], tgt_recv.at[k], plane_peer[k])
        for k in range(1, planes)
    ]
    to_team = [None] + [
        remote(own, src.at[2 * k], z_send.at[k], z_recv.at[k], team_peer[k])
        for k in range(1, teams)
    ]
    to_partner = [
        remote(own if k == 0 else src.at[2 * k], src.at[2 * k + 1], p_send.at[k], p_recv.at[k], partner)
        for k in range(teams)
    ]
    to_owner = [None] + [
        remote(grad_out.at[k - 1], grad_in.at[k - 1], g_send.at[k], g_recv.at[k], plane_peer[k])
        for k in range(1, planes)
    ]

    for load in loads:
        load.wait()
    pl.semaphore_wait(barrier, len(peers))
    to_partner[0].start()
    for k in range(1, teams):
        to_team[k].start()
    for k in range(1, planes):
        to_plane[k].start()

    def norm_of(ref):
        x = ref[0]
        xf = x.astype(jnp.float32)
        return x, jnp.sum(xf * xf, axis=1, keepdims=True)

    lane = lax.broadcasted_iota(jnp.int32, (rows, feat), 1)

    def raw_target(k):
        return own if k == 0 else tgt.at[k - 1]

    def raw_source(s):
        return own if s == 0 else src.at[s]

    def prepare_target(k):
        x, norm = norm_of(raw_target(k))
        tgt_aug[k, :, :feat] = x * jnp.bfloat16(-2.0)
        tgt_aug[k, :, feat:] = columns(norm, lane, 0, 3)

    def prepare_source(s):
        x, norm = norm_of(raw_source(s))
        src_aug[s, :, :feat] = x
        src_aug[s, :, feat:] = columns(norm, lane, 3, 0)

    def tile_pair(k, s, i, j, first):
        ti, sj = pl.ds(i, tile), pl.ds(j, tile)
        target, source = raw_target(k), raw_source(s)
        src_a = src_aug[s, sj, :]
        dist = lax.dot_general(tgt_aug[k, ti, :], src_a, NT, preferred_element_type=jnp.float32)
        couple = lax.dot_general(
            jnp.concatenate([target[1, ti, :], target[2, ti, :]], axis=1),
            jnp.concatenate([source[2, sj, :], source[1, sj, :]], axis=1),
            NT, preferred_element_type=jnp.float32,
        )
        dist = jnp.maximum(dist, 1e-30)
        power = dist * lax.rsqrt(dist) * (-RATE)
        weight = ((LOG2E - power) * jnp.exp2(power) * couple).astype(jnp.bfloat16)
        part = jnp.dot(weight, src_a, preferred_element_type=jnp.float32)
        if first:
            acc[k, ti, :] = part
        else:
            acc[k, ti, :] += part

    blocks = rows // tile

    def pair(k, s):
        if blocks == 1:
            tile_pair(k, s, 0, 0, s == 0)
            return

        @pl.loop(0, blocks)
        def _(i):
            i = pl.multiple_of(i * tile, tile)
            tile_pair(k, s, i, 0, s == 0)

            @pl.loop(1, blocks)
            def _(j):
                tile_pair(k, s, i, pl.multiple_of(j * tile, tile), False)

    def gradient(k):
        total = acc[k]
        x = raw_target(k)[0].astype(jnp.float32)
        return GAIN * (total[:, feat:feat + 1] * x - total[:, :feat])

    prepare_target(0)
    prepare_source(0)
    pair(0, 0)
    to_partner[0].wait_recv()
    prepare_source(1)
    pair(0, 1)
    if teams > 1:
        to_team[1].wait_recv()
        to_partner[1].start()
    for k in range(1, planes):
        to_plane[k].wait_recv()
        prepare_target(k)
        pair(k, 0)
        pair(k, 1)
    for z in range(1, teams):
        if z > 1:
            to_team[z].wait_recv()
            to_partner[z].start()
        prepare_source(2 * z)
        for k in range(planes):
            pair(k, 2 * z)
        to_partner[z].wait_recv()
        prepare_source(2 * z + 1)
        if z < teams - 1:
            for k in range(planes):
                pair(k, 2 * z + 1)
    for k in reversed(range(planes)):
        if teams > 1:
            pair(k, 2 * teams - 1)
        if k:
            grad_out[k - 1] = gradient(k).astype(jnp.bfloat16)
            to_owner[k].start()
    total = gradient(0)
    for k in reversed(range(1, planes)):
        to_owner[k].wait_recv()
        total += grad_in[k - 1].astype(jnp.float32)
    out_ref[...] = total
    for copy in to_plane[1:] + to_team[1:] + to_partner + to_owner[1:]:
        copy.wait_send()


def local(planes, teams, features, left_vectors, right_vectors):
    rows, feat = features.shape
    kind = jnp.bfloat16
    dma = pltpu.SemaphoreType.DMA
    tile = min(rows, 256)
    return pl.pallas_call(
        functools.partial(kernel, planes, teams, tile),
        out_shape=jax.ShapeDtypeStruct((rows, feat), jnp.float32),
        in_specs=[pl.BlockSpec(memory_space=pl.ANY)] * 3,
        out_specs=pl.BlockSpec(memory_space=pltpu.VMEM),
        scratch_shapes=[
            pltpu.VMEM((3, rows, feat), kind),
            pltpu.VMEM((max(planes - 1, 1), 3, rows, feat), kind),
            pltpu.VMEM((2 * teams, 3, rows, feat), kind),
            pltpu.VMEM((planes, rows, 2 * feat), kind),
            pltpu.VMEM((2 * teams, rows, 2 * feat), kind),
            pltpu.VMEM((planes, rows, 2 * feat), jnp.float32),
            pltpu.VMEM((max(planes - 1, 1), rows, feat), kind),
            pltpu.VMEM((max(planes - 1, 1), rows, feat), kind),
            dma((3,)),
            dma((planes,)), dma((planes,)),
            dma((teams,)), dma((teams,)),
            dma((teams,)), dma((teams,)),
            dma((planes,)), dma((planes,)),
        ],
        compiler_params=pltpu.CompilerParams(collective_id=0, has_side_effects=True),
    )(features, left_vectors, right_vectors)


def solution(mesh):
    spec = P(("blk", "team"), None)
    planes, teams = mesh.shape["blk"] // 2, mesh.shape["team"]
    return jax.shard_map(
        functools.partial(local, planes, teams), mesh=mesh,
        in_specs=(spec, spec, spec), out_specs=spec, check_vma=False,
    )
```

time: 130 us -> 32.4 us (0.25)
  blocking collectives: 75.4 us -> 0 us
  Pallas kernels: 0 us -> 30.6 us
  waiting for transfers between devices: 22.8 us -> 0 us
  matrix products: 16.3 us -> 0 us
  between operations: 13.4 us -> 0.01 us
    all_gather x6 -> x0, blocking collectives: 75.4 us -> none  [the longest x1 16 us: local(): lax.all_gather(features, 'team', axis=0, tiled=True)]
    pallas_call x0 -> x1, Pallas kernels: none -> 30.6 us  [local(): pl.pallas_call(functools.partial(kernel, planes, teams, tile), out_shape=...]
    reduce_scatter x1 -> x0, waiting for transfers between devices: 22.8 us -> none  [local(): lax.psum_scatter(partial_value, 'team', scatter_dimension=0, tiled=True)]
    dot_general x16 -> x0, matrix products: 16.3 us -> none  [the longest x4 10.1 us: pair_block(): jnp.einsum('iv,jv->ij', target_r, source_l, preferred_element_type=jnp.fl...]
  transfers between devices with their start and end apart: 1 -> 0, of which waited for: 1 -> 0; matrix products, arithmetic and copies ran while one was open for 0% -> 0% of each run, Pallas kernels for 0% -> 0%
where the time goes in v1:
time: 32.4 us; the launch traced here: 32.2 us
  Pallas kernels  30.6 us (94%)
  local copies, waits for them, and re-layouts  1.57 us (5%)
    pallas_call x1, Pallas kernels, local(): pl.pallas_call(functools.partial(kernel, planes, teams, tile), out_shape=...  30.6 us
    unnamed x1, local copies, waits for them, and re-layouts  1.57 us

profile of v1, /device:TPU:0, one launch (start us, length us, event | category | flops | bytes accessed | tf_op | source)
XLA Modules:
  0.0 32.2 jit_solution(16048026921704522424)
XLA Ops:
  0.0 30.6 %shard_map.37 = f32[256,128]{1,0:T(8,128)} custom-call(bf16[256,128]{1,0:T(8,128)(2,1)} %x_hbm.1, bf16[256,128]{1,0:T(8,128)(2,1)} %l_hbm.1, bf16[256,128]{1,0:T(8,128)(2,1)} %r_hbm.1), custom_call_target="tpu_custom_call" | custom-call | tf_op jit(solution)/shard_map/pallas_call | solution.py:203
  30.6 1.6 %copy.5 = f32[256,128]{1,0:T(8,128)} copy(f32[256,128]{1,0:T(8,128)} %shard_map.37) | data formatting | bytes 262144

commit v2 on v1

--- a/solution.py
+++ b/solution.py
@@ -36,7 +36,7 @@
 
 
 def kernel(
-    planes, teams, tile, x_hbm, l_hbm, r_hbm, out_ref,
+    planes, teams, tile, split, x_hbm, l_hbm, r_hbm, out_ref,
     own, tgt, src, tgt_aug, src_aug, acc, grad_out, grad_in,
     load_sem, tgt_send, tgt_recv, z_send, z_recv, p_send, p_recv, g_send, g_recv,
 ):
@@ -53,11 +53,14 @@
 
     partner = (plane * 2 + 1 - core, team)
     plane_peer = [(flip(plane, k) * 2 + core, team) for k in range(planes)]
-    team_peer = [(blk, flip(team, k)) for k in range(teams)]
-    peers = [partner] + plane_peer[1:] + team_peer[1:]
+    peers = [partner] + plane_peer[1:]
     barrier = pltpu.get_barrier_semaphore()
     for peer in peers:
         pl.semaphore_signal(barrier, inc=1, device_id=peer, device_id_type=MESH)
+    for step in (1, -1):
+        @pl.when((team + step >= 0) & (team + step < teams))
+        def _():
+            pl.semaphore_signal(barrier, inc=1, device_id=(blk, team + step), device_id_type=MESH)
 
     def remote(source, target, send, recv, peer):
         return pltpu.make_async_remote_copy(
@@ -69,14 +72,46 @@
         remote(own, tgt.at[k - 1], tgt_send.at[k], tgt_recv.at[k], plane_peer[k])
         for k in range(1, planes)
     ]
-    to_team = [None] + [
-        remote(own, src.at[2 * k], z_send.at[k], z_recv.at[k], team_peer[k])
-        for k in range(1, teams)
-    ]
-    to_partner = [
-        remote(own if k == 0 else src.at[2 * k], src.at[2 * k + 1], p_send.at[k], p_recv.at[k], partner)
-        for k in range(teams)
-    ]
+    size = rows // split
+    left, right = team, teams - 1 - team
+    both = jnp.minimum(left, right)
+
+    def position(n):
+        paired = n <= 2 * both
+        far = jnp.where(paired, (n + 1) // 2, n - both)
+        sign = jnp.where(paired, 1 - 2 * (n % 2), jnp.where(left < right, 1, -1))
+        return team + sign * far, -sign
+
+    order = [None] + [position(n) for n in range(1, teams)]
+
+    def part_of(ref, h):
+        return ref.at[:, pl.ds(h * size, size)]
+
+    def line_copy(source, shard, h, send, step):
+        return remote(
+            part_of(source, h), part_of(src.at[2 * shard], h), send, z_recv.at[shard, h],
+            (blk, team + step),
+        )
+
+    def can_go(step):
+        return (team + step >= 0) & (team + step < teams)
+
+    def own_copy(step, h):
+        return line_copy(own, team, h, z_send.at[team if step > 0 else teams, h], step)
+
+    def forward(n, h):
+        shard, step = order[n]
+        return line_copy(src.at[2 * shard], shard, h, z_send.at[shard, h], step)
+
+    def relay(n, h):
+        shard = order[n][0]
+        return remote(
+            part_of(src.at[2 * shard], h), part_of(src.at[2 * shard + 1], h),
+            p_send.at[shard, h], p_recv.at[shard, h], partner,
+        )
+
+    mine = 2 * team
+    to_partner = remote(own, src.at[mine + 1], p_send.at[team, 0], p_recv.at[team, 0], partner)
     to_owner = [None] + [
         remote(grad_out.at[k - 1], grad_in.at[k - 1], g_send.at[k], g_recv.at[k], plane_peer[k])
         for k in range(1, planes)
@@ -84,35 +119,39 @@
 
     for load in loads:
         load.wait()
-    pl.semaphore_wait(barrier, len(peers))
-    to_partner[0].start()
-    for k in range(1, teams):
-        to_team[k].start()
+    on_line = jnp.minimum(team, 1) + jnp.minimum(teams - 1 - team, 1)
+    pl.semaphore_wait(barrier, len(peers) + on_line)
+    to_partner.start()
+    for h in range(split):
+        for step in (1, -1):
+            @pl.when(can_go(step))
+            def _():
+                own_copy(step, h).start()
     for k in range(1, planes):
         to_plane[k].start()
 
-    def norm_of(ref):
-        x = ref[0]
+    def norm_of(x):
         xf = x.astype(jnp.float32)
-        return x, jnp.sum(xf * xf, axis=1, keepdims=True)
-
-    lane = lax.broadcasted_iota(jnp.int32, (rows, feat), 1)
+        return jnp.sum(xf * xf, axis=1, keepdims=True)
+
 
     def raw_target(k):
         return own if k == 0 else tgt.at[k - 1]
 
     def raw_source(s):
-        return own if s == 0 else src.at[s]
+        return own if s is mine else src.at[s]
+
+    lane = lax.broadcasted_iota(jnp.int32, (rows, feat), 1)
 
     def prepare_target(k):
-        x, norm = norm_of(raw_target(k))
+        x = raw_target(k)[0]
         tgt_aug[k, :, :feat] = x * jnp.bfloat16(-2.0)
-        tgt_aug[k, :, feat:] = columns(norm, lane, 0, 3)
+        tgt_aug[k, :, feat:] = columns(norm_of(x), lane, 0, 3)
 
     def prepare_source(s):
-        x, norm = norm_of(raw_source(s))
+        x = raw_source(s)[0]
         src_aug[s, :, :feat] = x
-        src_aug[s, :, feat:] = columns(norm, lane, 3, 0)
+        src_aug[s, :, feat:] = columns(norm_of(x), lane, 3, 0)
 
     def tile_pair(k, s, i, j, first):
         ti, sj = pl.ds(i, tile), pl.ds(j, tile)
@@ -133,19 +172,17 @@
         else:
             acc[k, ti, :] += part
 
-    blocks = rows // tile
-
     def pair(k, s):
-        if blocks == 1:
-            tile_pair(k, s, 0, 0, s == 0)
+        if rows == tile:
+            tile_pair(k, s, 0, 0, s is mine)
             return
 
-        @pl.loop(0, blocks)
+        @pl.loop(0, rows // tile)
         def _(i):
             i = pl.multiple_of(i * tile, tile)
-            tile_pair(k, s, i, 0, s == 0)
-
-            @pl.loop(1, blocks)
+            tile_pair(k, s, i, 0, s is mine)
+
+            @pl.loop(1, rows // tile)
             def _(j):
                 tile_pair(k, s, i, pl.multiple_of(j * tile, tile), False)
 
@@ -154,35 +191,74 @@
         x = raw_target(k)[0].astype(jnp.float32)
         return GAIN * (total[:, feat:feat + 1] * x - total[:, :feat])
 
+    inner = both > 0
+
+    def receive(n, h):
+        line_copy(own, order[n][0], h, z_send.at[0, 0], 0).wait_recv()
+
+        @pl.when(can_go(order[n][1]))
+        def _():
+            forward(n, h).start()
+        relay(n, h).start()
+
+    def receive_when(condition, n, halves=range(split)):
+        if n < teams:
+            @pl.when(condition)
+            def _():
+                for h in halves:
+                    receive(n, h)
+
+    def take(n):
+        prepare_source(2 * order[n][0])
+        return 2 * order[n][0]
+
+    def take_partner(n):
+        for h in range(split):
+            relay(n, h).wait_recv()
+        prepare_source(2 * order[n][0] + 1)
+        return 2 * order[n][0] + 1
+
     prepare_target(0)
-    prepare_source(0)
-    pair(0, 0)
-    to_partner[0].wait_recv()
-    prepare_source(1)
-    pair(0, 1)
+    prepare_source(mine)
+    pair(0, mine)
+    to_partner.wait_recv()
+    next_door = mine + 1
+    prepare_source(next_door)
+    pair(0, next_door)
     if teams > 1:
-        to_team[1].wait_recv()
-        to_partner[1].start()
+        for h in range(split):
+            receive(1, h)
+        receive_when(inner, 2)
+        first = take(1)
+        pair(0, first)
     for k in range(1, planes):
         to_plane[k].wait_recv()
+        if k == planes - 1:
+            receive_when(inner, 3)
         prepare_target(k)
-        pair(k, 0)
-        pair(k, 1)
-    for z in range(1, teams):
-        if z > 1:
-            to_team[z].wait_recv()
-            to_partner[z].start()
-        prepare_source(2 * z)
+        pair(k, mine)
+        pair(k, next_door)
+        if teams > 1:
+            pair(k, first)
+    outer = jnp.logical_not(inner)
+    receive_when(outer, 2)
+    for n in range(1, teams - 1):
+        slot = take_partner(n)
         for k in range(planes):
-            pair(k, 2 * z)
-        to_partner[z].wait_recv()
-        prepare_source(2 * z + 1)
-        if z < teams - 1:
-            for k in range(planes):
-                pair(k, 2 * z + 1)
+            pair(k, slot)
+        if n + 1 > 3:
+            for h in range(split):
+                receive(n + 1, h)
+        elif n + 1 == 3:
+            receive_when(outer, 3)
+        slot = take(n + 1)
+        for k in range(planes):
+            pair(k, slot)
+    if teams > 1:
+        slot = take_partner(teams - 1)
     for k in reversed(range(planes)):
         if teams > 1:
-            pair(k, 2 * teams - 1)
+            pair(k, slot)
         if k:
             grad_out[k - 1] = gradient(k).astype(jnp.bfloat16)
             to_owner[k].start()
@@ -191,17 +267,28 @@
         to_owner[k].wait_recv()
         total += grad_in[k - 1].astype(jnp.float32)
     out_ref[...] = total
-    for copy in to_plane[1:] + to_team[1:] + to_partner + to_owner[1:]:
+    for copy in to_plane[1:] + [to_partner] + to_owner[1:]:
         copy.wait_send()
+    for h in range(split):
+        for step in (1, -1):
+            @pl.when(can_go(step))
+            def _():
+                own_copy(step, h).wait_send()
+        for n in range(1, teams):
+            relay(n, h).wait_send()
+
+            @pl.when(can_go(order[n][1]))
+            def _():
+                forward(n, h).wait_send()
 
 
 def local(planes, teams, features, left_vectors, right_vectors):
     rows, feat = features.shape
     kind = jnp.bfloat16
     dma = pltpu.SemaphoreType.DMA
-    tile = min(rows, 256)
+    tile, split = min(rows, 256), 2
     return pl.pallas_call(
-        functools.partial(kernel, planes, teams, tile),
+        functools.partial(kernel, planes, teams, tile, split),
         out_shape=jax.ShapeDtypeStruct((rows, feat), jnp.float32),
         in_specs=[pl.BlockSpec(memory_space=pl.ANY)] * 3,
         out_specs=pl.BlockSpec(memory_space=pltpu.VMEM),
@@ -216,8 +303,8 @@
             pltpu.VMEM((max(planes - 1, 1), rows, feat), kind),
             dma((3,)),
             dma((planes,)), dma((planes,)),
-            dma((teams,)), dma((teams,)),
-            dma((teams,)), dma((teams,)),
+            dma((teams + 1, split)), dma((teams, split)),
+            dma((teams, split)), dma((teams, split)),
             dma((planes,)), dma((planes,)),
         ],
         compiler_params=pltpu.CompilerParams(collective_id=0, has_side_effects=True),

time: 32.4 us -> 29.4 us (0.907)
  Pallas kernels: 30.6 us -> 27.6 us
    pallas_call x1, Pallas kernels: 30.6 us -> 27.6 us  [local(): pl.pallas_call(functools.partial(kernel, planes, teams, tile, split), out...]
where the time goes in v2:
time: 29.4 us; the launch traced here: 29.2 us
  Pallas kernels  27.6 us (94%)
  local copies, waits for them, and re-layouts  1.57 us (5%)
    pallas_call x1, Pallas kernels, local(): pl.pallas_call(functools.partial(kernel, planes, teams, tile, split), out...  27.6 us
    unnamed x1, local copies, waits for them, and re-layouts  1.57 us

profile of v2, /device:TPU:0, one launch (start us, length us, event | category | flops | bytes accessed | tf_op | source)
XLA Modules:
  0.0 29.2 jit_solution(16638451133788188469)
XLA Ops:
  0.0 27.6 %shard_map.37 = f32[256,128]{1,0:T(8,128)} custom-call(bf16[256,128]{1,0:T(8,128)(2,1)} %x_hbm.1, bf16[256,128]{1,0:T(8,128)(2,1)} %l_hbm.1, bf16[256,128]{1,0:T(8,128)(2,1)} %r_hbm.1), custom_call_target="tpu_custom_call" | custom-call | tf_op jit(solution)/shard_map/pallas_call | solution.py:290
  27.7 1.6 %copy.5 = f32[256,128]{1,0:T(8,128)} copy(f32[256,128]{1,0:T(8,128)} %shard_map.37) | data formatting | bytes 262144

commit v3 on v2

--- a/solution.py
+++ b/solution.py
@@ -36,8 +36,8 @@
 
 
 def kernel(
-    planes, teams, tile, split, x_hbm, l_hbm, r_hbm, out_ref,
-    own, tgt, src, tgt_aug, src_aug, acc, grad_out, grad_in,
+    planes, teams, tile, split, x_hbm, l_hbm, r_hbm, out_ref, grad_in,
+    own, tgt, src, tgt_aug, src_aug, acc, grad_out, mine_out, out_sem,
     load_sem, tgt_send, tgt_recv, z_send, z_recv, p_send, p_recv, g_send, g_recv,
 ):
     blk, team = lax.axis_index("blk"), lax.axis_index("team")
@@ -262,11 +262,12 @@
         if k:
             grad_out[k - 1] = gradient(k).astype(jnp.bfloat16)
             to_owner[k].start()
-    total = gradient(0)
+    mine_out[...] = gradient(0)
+    put = pltpu.make_async_copy(mine_out, out_ref, out_sem)
+    put.start()
     for k in reversed(range(1, planes)):
         to_owner[k].wait_recv()
-        total += grad_in[k - 1].astype(jnp.float32)
-    out_ref[...] = total
+    put.wait()
     for copy in to_plane[1:] + [to_partner] + to_owner[1:]:
         copy.wait_send()
     for h in range(split):
@@ -287,11 +288,14 @@
     kind = jnp.bfloat16
     dma = pltpu.SemaphoreType.DMA
     tile, split = min(rows, 256), 2
-    return pl.pallas_call(
+    partial, received = pl.pallas_call(
         functools.partial(kernel, planes, teams, tile, split),
-        out_shape=jax.ShapeDtypeStruct((rows, feat), jnp.float32),
+        out_shape=(
+            jax.ShapeDtypeStruct((rows, feat), jnp.float32),
+            jax.ShapeDtypeStruct((max(planes - 1, 1), rows, feat), kind),
+        ),
         in_specs=[pl.BlockSpec(memory_space=pl.ANY)] * 3,
-        out_specs=pl.BlockSpec(memory_space=pltpu.VMEM),
+        out_specs=(pl.BlockSpec(memory_space=pl.ANY),) * 2,
         scratch_shapes=[
             pltpu.VMEM((3, rows, feat), kind),
             pltpu.VMEM((max(planes - 1, 1), 3, rows, feat), kind),
@@ -300,7 +304,8 @@
             pltpu.VMEM((2 * teams, rows, 2 * feat), kind),
             pltpu.VMEM((planes, rows, 2 * feat), jnp.float32),
             pltpu.VMEM((max(planes - 1, 1), rows, feat), kind),
-            pltpu.VMEM((max(planes - 1, 1), rows, feat), kind),
+            pltpu.VMEM((rows, feat), jnp.float32),
+            dma,
             dma((3,)),
             dma((planes,)), dma((planes,)),
             dma((teams + 1, split)), dma((teams, split)),
@@ -309,6 +314,9 @@
         ],
         compiler_params=pltpu.CompilerParams(collective_id=0, has_side_effects=True),
     )(features, left_vectors, right_vectors)
+    for k in range(planes - 1):
+        partial = partial + received[k].astype(jnp.float32)
+    return partial
 
 
 def solution(mesh):

time: 29.4 us -> 28.9 us (0.983)
  other arithmetic: 0 us -> 1.65 us
  local copies, waits for them, and re-layouts: 1.57 us -> 0 us
  Pallas kernels: 27.6 us -> 27.1 us
    add x0 -> x1, other arithmetic: none -> 1.65 us  [local(): partial = partial + received[k].astype(jnp.float32)]
    unnamed x1 -> x0, local copies, waits for them, and re-layouts: 1.57 us -> none
    pallas_call x1, Pallas kernels: 27.6 us -> 27.1 us  [local(): pl.pallas_call(functools.partial(kernel, planes, teams, tile, split), out...]
where the time goes in v3:
time: 28.9 us; the launch traced here: 28.8 us
  Pallas kernels  27.1 us (94%)
  other arithmetic  1.65 us (6%)
    pallas_call x1, Pallas kernels, local(): pl.pallas_call(functools.partial(kernel, planes, teams, tile, split), out...  27.1 us
    add x1, other arithmetic, local(): partial = partial + received[k].astype(jnp.float32)  1.65 us

profile of v3, /device:TPU:0, one launch (start us, length us, event | category | flops | bytes accessed | tf_op | source)
XLA Modules:
  0.0 28.8 jit_solution(13140066107309516952)
XLA Ops:
  0.0 27.1 %shard_map.37 = (f32[256,128]{1,0:T(8,128)}, bf16[3,256,128]{2,1,0:T(8,128)(2,1)}) custom-call(bf16[256,128]{1,0:T(8,128)(2,1)} %x_hbm.1, bf16[256,128]{1,0:T(8,128)(2,1)} %l_hbm.1, bf16[256,128]{1,0:T(8,128)(2,1)} %r_hbm.1), custom_call_target="tpu_custom_call" | custom-call | tf_op jit(solution)/shard_map/pallas_call | solution.py:291
  27.1 1.7 %convert_add_fusion = f32[256,128]{1,0:T(8,128)} fusion(f32[256,128]{1,0:T(8,128)} %get-tuple-element.7, bf16[3,256,128]{2,1,0:T(8,128)(2,1)} %get-tuple-element.8), kind=kLoop, calls=%fused_computation | loop fusion | flops 196608 | bytes 458752 | tf_op jit(solution)/shard_map/add | solution.py:318
